TPU v7x, 32 devices: a whole 2x2x4 slice. The times are simulated.
32 devices in a mesh: groups: 2 (over y), expert: 4 (over x, core), tensor: 4 (over z).
Axes of the slice: x: 2, y: 2, z: 4, core: 2. Of those that a mesh axis runs over, the one named last changes fastest.
Arguments:
- tokens: bfloat16 [2048, 2048], P(('groups', 'expert')), parts along dimension 0, may hold values from -6 to 6
- route_ids: int32 [2048, 2], P(('groups', 'expert')), parts along dimension 0, may hold values from 0 to 3, all different within a row; in each aligned block of 256 rows (0 to 255, 256 to 511, ...) at most 256 rows name the same one
- route_weights: float32 [2048, 2], P(('groups', 'expert')), parts along dimension 0, may hold values from 0.2 to 1
- modulation: float32 [8, 6144], P(('groups', 'expert')), parts along dimension 0, may hold values from -5 to 5
- partner: int32 [4], replicated, may hold values from 0 to 3, as said below
- w_gate: bfloat16 [4, 2048, 4096], P('expert', None, 'tensor'), may hold values from -0.125 to 0.125
- w_up: bfloat16 [4, 2048, 4096], P('expert', None, 'tensor'), may hold values from -0.125 to 0.125
- w_down: bfloat16 [4, 4096, 2048], P('expert', 'tensor'), may hold values from -0.09375 to 0.09375
- spare_gate: bfloat16 [4, 2048, 4096], P('expert', None, 'tensor'), may hold values from -0.125 to 0.125
- spare_up: bfloat16 [4, 2048, 4096], P('expert', None, 'tensor'), may hold values from -0.125 to 0.125
- spare_down: bfloat16 [4, 4096, 2048], P('expert', 'tensor'), may hold values from -0.09375 to 0.09375
Outputs:
- layer_out: bfloat16 [2048, 2048], P(('groups', 'expert'), 'tensor'), parts along dimension 0
There are 2 independent parts, one for each index of `groups`. A program takes and returns all parts, laid end to end along the dimension named above; an argument that names none is the same for every part. Nothing has to cross between parts.
Inputs may be any that keep to these rules, and one draw needn't show every extreme that they name: `route_ids`: the two ids of a token differ. Within the 256 tokens of one image no expert is named more than 2 * 128 times; in some image some expert is named exactly 2 * 128 times. partner is a permutation of the experts with partner[e] != e for every e.
All inputs are finite; a program needn't handle non-finite values.
Results may differ from a plain program's by a relative error of at most 0.014.
Values may be sent and summed in bfloat16 or wider, within the bound.
No kernel may reach another device: no remote copies, remote signals or barrier semaphores. Data moves between devices by JAX's collectives and lax.ppermute only.
A program may use at most 64 MiB of HBM per device.

v0:
```python
import jax
import jax.numpy as jnp
from jax import lax
from jax.sharding import PartitionSpec as P


def slot_targets(ids, partner, experts, capacity):
    flat = ids.reshape(-1)
    onehot = (flat[:, None] == jnp.arange(experts, dtype=jnp.int32)[None, :]).astype(jnp.int32)
    ranks = jnp.sum((jnp.cumsum(onehot, axis=0) - 1) * onehot, axis=1)
    spare_of = jnp.sum(onehot * partner[None, :], axis=1)
    server = jnp.where(ranks >= capacity, spare_of, flat)
    return server * (2 * capacity) + ranks


def per_device(
    tokens,
    route_ids,
    route_weights,
    modulation,
    partner,
    w_gate,
    w_up,
    w_down,
    spare_gate,
    spare_up,
    spare_down,
):
    experts = lax.axis_size("expert")
    shards = lax.axis_size("tensor")
    rows, width = tokens.shape
    capacity = 2 * rows // experts
    columns = width // shards
    mod_row = modulation[0]
    tensor_start = lax.axis_index("tensor") * columns
    values = tokens.astype(jnp.float32)
    mean = jnp.mean(values, axis=1, keepdims=True)
    centred = values - mean
    var = jnp.mean(centred * centred, axis=1, keepdims=True)
    normed = centred / jnp.sqrt(var + 1e-06)
    modded = (normed * (1.0 + mod_row[width : 2 * width]) + mod_row[0:width]).astype(jnp.bfloat16)
    targets = slot_targets(route_ids, partner, experts, capacity)
    features = modded.shape[1]
    spread = jnp.repeat(modded, 2, axis=0)
    outgoing = jnp.zeros((experts * 2 * capacity, features), jnp.bfloat16).at[targets].set(spread)
    outgoing = outgoing.reshape(experts, 2, capacity, features)
    home_set = (w_gate[0], w_up[0], w_down[0])
    spare_set = (spare_gate[0], spare_up[0], spare_down[0])

    def project(block, weight_sets):
        count = block.shape[2]
        which = 0
        weight_set = weight_sets[which]
        flat_rows = block[:, which].reshape(experts * count, width)
        gate_sum = jnp.dot(flat_rows, weight_set[0], preferred_element_type=jnp.float32)
        up_sum = jnp.dot(flat_rows, weight_set[1], preferred_element_type=jnp.float32)
        products = [(gate_sum, up_sum)]
        which = 0
        gate_sum, up_sum = products[which]
        hidden = (jax.nn.silu(gate_sum) * up_sum).astype(jnp.bfloat16)
        rounded = jnp.dot(hidden, weight_sets[which][2], preferred_element_type=jnp.float32).astype(
            jnp.bfloat16
        )
        pieces = rounded.astype(jnp.float32).reshape(experts, 1, count, width)
        shares = lax.psum_scatter(
            pieces.astype(jnp.bfloat16), "tensor", scatter_dimension=3, tiled=True
        ).astype(jnp.float32)
        return lax.all_to_all(
            shares.astype(jnp.bfloat16), "expert", split_axis=0, concat_axis=0, tiled=True
        ).astype(shares.dtype)

    home_back = project(
        lax.all_to_all(outgoing[:, 0:1], "expert", split_axis=0, concat_axis=0, tiled=True),
        (home_set,),
    )
    spill_back = project(
        lax.all_to_all(outgoing[:, 1:2], "expert", split_axis=0, concat_axis=0, tiled=True),
        (spare_set,),
    )
    returned = jnp.concatenate((home_back, spill_back), axis=1)
    flat_back = returned.reshape(experts * 2 * capacity, columns)
    picked = flat_back[targets].reshape(rows, 2, columns)
    mixed = jnp.sum(picked * route_weights[:, :, None], axis=1)
    own_cols = lax.dynamic_slice_in_dim(values, tensor_start, columns, 1)
    gate_cols = lax.dynamic_slice_in_dim(mod_row, 2 * width + tensor_start, columns, 0)
    return (own_cols + gate_cols[None, :] * mixed).astype(jnp.bfloat16)


def solution(mesh):
    placed = (
        P(("groups", "expert"), None),
        P(("groups", "expert"), None),
        P(("groups", "expert"), None),
        P(("groups", "expert"), None),
        P(),
        P("expert", None, "tensor"),
        P("expert", None, "tensor"),
        P("expert", "tensor", None),
        P("expert", None, "tensor"),
        P("expert", None, "tensor"),
        P("expert", "tensor", None),
    )
    return jax.shard_map(
        per_device,
        mesh=mesh,
        in_specs=placed,
        out_specs=P(("groups", "expert"), "tensor"),
        check_vma=False,
    )
```

profile of v0, /device:TPU:0, one launch (start us, length us, event | category | flops | bytes accessed | tf_op | source)
XLA Modules:
  0.0 186.0 jit_solution(12211462042598215440)
XLA Ops:
  6.5 0.0 copy-start
  6.5 0.0 reduce-scatter.3.cloned.1.call-start
  6.5 0.9 copy.19
  7.4 0.1 eq.29
  7.6 0.1 eq.25
  7.7 0.1 reshape.121
  7.9 1.2 reduce-window.6
  9.1 0.2 slice_reduce_fusion
  9.3 0.2 reduce-window.9
  9.5 0.1 add_bitcast_fusion
  9.6 0.7 slice_add_fusion
  10.3 1.4 convert_reduce_fusion
  11.8 0.0 copy-done
  11.8 0.4 multiply_reduce_fusion
  12.2 0.5 add_convert_fusion
  12.7 1.3 broadcast_in_dim.5
  14.0 0.0 copy-start.4
  14.0 2.2 %reshape.141 = bf16[512,2048]{1,0:T(8,128)(2,1)} reshape(bf16[256,2,2048]{2,1,0:T(2,128)(2,1)S(1)} %broadcast_in_dim.5) | data formatting | bytes 4194304 | tf_op jit(solution)/shard_map/reshape | solution.py:44
  16.2 0.0 copy-done.4
  16.2 0.1 select_reduce_fusion
  16.3 7.2 %scatter_custom_fusion = bf16[1024,2048]{1,0:T(8,128)(2,1)} fusion(s32[512]{0:T(512)S(1)} %bitcast.78, bf16[512,2048]{1,0:T(8,128)(2,1)} %reshape.141, bf16[]{:T(256)} %constant.14.clone.1), kind=kCustom, calls=%fused_computation.20 | custom fusion | bytes 4194816 | tf_op jit(solution)/shard_map/scatter | solution.py:45
  23.5 2.6 %fusion.35 = (bf16[4,1,128,2048]{3,2,1,0:T(8,128)(2,1)S(1)}, bf16[4,1,128,2048]{3,2,1,0:T(8,128)(2,1)S(1)}) fusion(bf16[4,2,128,2048]{3,2,1,0:T(8,128)(2,1)} %bitcast.67), kind=kLoop, calls=%fused_computation.47 | loop fusion | bytes 8388608 | tf_op jit(solution)/shard_map/slice | solution.py:73
  26.2 0.0 copy-start.5
  26.2 30.0 %all_to_all.20 = bf16[4,1,128,2048]{3,2,1,0:T(8,128)(2,1)S(1)} all-to-all(bf16[4,1,128,2048]{3,2,1,0:T(8,128)(2,1)S(1)} %get-tuple-element.7), channel_id=1, replica_groups=mesh['groups'=2,'expert'=4,'tensor'=4] {'expert'}, dimensions={0} | all-to-all | bytes 4194304 | tf_op jit(solution)/shard_map/all_to_all | solution.py:73
  56.1 0.0 copy-start.1
  56.2 1.3 copy-done.1
  57.5 0.0 copy-done.5
  57.5 3.6 %fusion.10 = f32[512,1024]{1,0:T(8,128)} fusion(bf16[512,2048]{1,0:T(8,128)(2,1)S(1)} %bitcast.70, bf16[1,2048,1024]{2,1,0:T(8,128)(2,1)S(1)} %copy-done.5), kind=kOutput, calls=%fused_computation.12 | convolution fusion | flops 2147483648 | bytes 8388608 | tf_op jit(solution)/shard_map/dot_general | solution.py:55
  61.1 10.6 %fusion.12 = bf16[512,2048]{1,0:T(8,128)(2,1)} fusion(bf16[1,1024,2048]{2,1,0:T(8,128)(2,1)} %param.18, f32[512,1024]{1,0:T(8,128)} %fusion.10, bf16[512,2048]{1,0:T(8,128)(2,1)} %bitcast.71, bf16[1,2048,1024]{2,1,0:T(8,128)(2,1)} %param.17), kind=kOutput, calls=%fused_computation.14 | convolution fusion | flops 4299161600 | bytes 14680064 | tf_op jit(solution)/shard_map/dot_general | solution.py:61
  71.7 0.0 reduce-scatter.3.cloned.1.call-update
  71.7 0.0 reduce-scatter.5.cloned.1.call-start
  71.8 0.0 copy-start.6
  71.8 28.4 %all_to_all.21 = bf16[4,1,128,2048]{3,2,1,0:T(8,128)(2,1)S(1)} all-to-all(bf16[4,1,128,2048]{3,2,1,0:T(8,128)(2,1)S(1)} %get-tuple-element.8), channel_id=1, replica_groups=mesh['groups'=2,'expert'=4,'tensor'=4] {'expert'}, dimensions={0} | all-to-all | bytes 4194304 | tf_op jit(solution)/shard_map/all_to_all | solution.py:77
  100.2 0.0 copy-start.2
  100.2 1.3 copy-done.2
  101.5 0.0 copy-done.6
  101.5 2.3 %fusion.4 = f32[512,1024]{1,0:T(8,128)S(1)} fusion(bf16[512,2048]{1,0:T(8,128)(2,1)S(1)} %bitcast.72, bf16[1,2048,1024]{2,1,0:T(8,128)(2,1)S(1)} %copy-done.6), kind=kOutput, calls=%fused_computation.6 | convolution fusion | flops 2147483648 | bytes 8388608 | tf_op jit(solution)/shard_map/dot_general | solution.py:55
  103.9 10.0 %fusion.15 = bf16[512,2048]{1,0:T(8,128)(2,1)} fusion(bf16[1,1024,2048]{2,1,0:T(8,128)(2,1)} %param.21, f32[512,1024]{1,0:T(8,128)S(1)} %fusion.4, bf16[512,2048]{1,0:T(8,128)(2,1)} %bitcast.73, bf16[1,2048,1024]{2,1,0:T(8,128)(2,1)} %param.20), kind=kOutput, calls=%fused_computation.15 | convolution fusion | flops 4299161600 | bytes 14680064 | tf_op jit(solution)/shard_map/dot_general | solution.py:61
  113.9 0.0 reduce-scatter.5.cloned.1.call-update
  113.9 2.0 %reduce-scatter.3.cloned.1.call-done = bf16[4,1,128,512]{3,2,1,0:T(8,128)(2,1)} async-done(((bf16[4,1,128,2048]{3,2,1,0:T(8,128)(2,1)}), bf16[4,1,128,512]{3,2,1,0:T(8,128)(2,1)}) %reduce-scatter.3.cloned.1.call-update) | async-done | bytes 524304 | tf_op jit(solution)/shard_map/reduce_scatter | solution.py:65
  115.8 3.5 %all-to-all-start.1 = ((bf16[4,1,128,512]{3,2,1,0:T(8,128)(2,1)}), bf16[4,1,128,512]{3,2,1,0:T(8,128)(2,1)S(1)}, u32[]{:S(2)}, u32[]{:S(2)}) async-start(bf16[4,1,128,512]{3,2,1,0:T(8,128)(2,1)} %reduce-scatter.3.cloned.1.call-done), calls=%async_computation.2 | async-start | bytes 1048576 | tf_op jit(solution)/shard_map/all_to_all | solution.py:68
  119.3 0.0 copy-start.3
  119.3 41.7 %reduce-scatter.5.cloned.1.call-done = bf16[4,1,128,512]{3,2,1,0:T(8,128)(2,1)} async-done(((bf16[4,1,128,2048]{3,2,1,0:T(8,128)(2,1)}), bf16[4,1,128,512]{3,2,1,0:T(8,128)(2,1)}) %reduce-scatter.5.cloned.1.call-update) | async-done | bytes 524304 | tf_op jit(solution)/shard_map/reduce_scatter | solution.py:65
  161.0 0.0 all-to-all-done.1
  161.0 3.7 %all-to-all-start.3 = ((bf16[4,1,128,512]{3,2,1,0:T(8,128)(2,1)}), bf16[4,1,128,512]{3,2,1,0:T(8,128)(2,1)S(1)}, u32[]{:S(2)}, u32[]{:S(2)}) async-start(bf16[4,1,128,512]{3,2,1,0:T(8,128)(2,1)} %reduce-scatter.5.cloned.1.call-done), calls=%async_computation.5 | async-start | bytes 1048576 | tf_op jit(solution)/shard_map/all_to_all | solution.py:68
  164.7 1.6 convert_element_type.58
  166.3 0.0 copy-done.3
  166.3 0.1 copy.24
  166.5 0.7 constant_dynamic-slice_fusion
  167.2 6.1 %all-to-all-done.3 = bf16[4,1,128,512]{3,2,1,0:T(8,128)(2,1)S(1)} async-done(((bf16[4,1,128,512]{3,2,1,0:T(8,128)(2,1)}), bf16[4,1,128,512]{3,2,1,0:T(8,128)(2,1)S(1)}, u32[]{:S(2)}, u32[]{:S(2)}) %all-to-all-start.3) | async-done | bytes 524320 | tf_op jit(solution)/shard_map/all_to_all | solution.py:68
  173.3 0.1 pad_maximum_fusion
  173.4 0.3 bitcast_convert_fusion
  173.7 1.6 gather_fusion
  175.4 0.6 reshape.126
  176.0 1.3 multiply_reduce_fusion.1
  177.3 1.9 add_convert_fusion.1
  (5 shorter events, 0.0 us)
Async XLA Ops:
  6.5 5.2 %copy-start = (bf16[256,2048]{1,0:T(8,128)(2,1)S(1)}, bf16[256,2048]{1,0:T(8,128)(2,1)}, u32[]{:S(2)}) copy-start(bf16[256,2048]{1,0:T(8,128)(2,1)} %param.11) | copy-start | bytes 3145732
  6.5 109.3 %reduce-scatter.3.cloned.1.call-start = ((), (), s32[]{:S(2)}) async-start(), calls=%async_computation.6 | async-start | bytes 2621440 | tf_op jit(solution)/shard_map/reduce_scatter | solution.py:65
  14.0 2.3 %copy-start.4 = (s32[4]{0:T(128)S(1)}, s32[4]{0:T(128)}, u32[]{:S(2)}) copy-start(s32[4]{0:T(128)} %param.15) | copy-start | bytes 52
  26.2 31.3 %copy-start.5 = (bf16[1,2048,1024]{2,1,0:T(8,128)(2,1)S(1)}, bf16[1,2048,1024]{2,1,0:T(8,128)(2,1)}, u32[]{:S(2)}) copy-start(bf16[1,2048,1024]{2,1,0:T(8,128)(2,1)} %param.16) | copy-start | bytes 12582916
  56.1 1.3 copy-start.1
  71.7 89.3 %reduce-scatter.5.cloned.1.call-start = ((), (), s32[]{:S(2)}) async-start(), calls=%async_computation.7 | async-start | bytes 2621440 | tf_op jit(solution)/shard_map/reduce_scatter | solution.py:65
  71.8 29.7 %copy-start.6 = (bf16[1,2048,1024]{2,1,0:T(8,128)(2,1)S(1)}, bf16[1,2048,1024]{2,1,0:T(8,128)(2,1)}, u32[]{:S(2)}) copy-start(bf16[1,2048,1024]{2,1,0:T(8,128)(2,1)} %param.19) | copy-start | bytes 12582916
  100.2 1.3 copy-start.2
  115.8 45.2 %all-to-all-start.1 = ((bf16[4,1,128,512]{3,2,1,0:T(8,128)(2,1)}), bf16[4,1,128,512]{3,2,1,0:T(8,128)(2,1)S(1)}, u32[]{:S(2)}, u32[]{:S(2)}) async-start(bf16[4,1,128,512]{3,2,1,0:T(8,128)(2,1)} %reduce-scatter.3.cloned.1.call-done), calls=%async_computation.2 | async-start | bytes 1048576 | tf_op jit(solution)/shard_map/all_to_all | solution.py:68
  119.3 47.0 %copy-start.3 = (f32[256,2]{0,1:T(2,128)S(1)}, f32[256,2]{0,1:T(2,128)}, u32[]{:S(2)}) copy-start(f32[256,2]{0,1:T(2,128)} %param.13) | copy-start | bytes 6148
  161.0 12.3 %all-to-all-start.3 = ((bf16[4,1,128,512]{3,2,1,0:T(8,128)(2,1)}), bf16[4,1,128,512]{3,2,1,0:T(8,128)(2,1)S(1)}, u32[]{:S(2)}, u32[]{:S(2)}) async-start(bf16[4,1,128,512]{3,2,1,0:T(8,128)(2,1)} %reduce-scatter.5.cloned.1.call-done), calls=%async_computation.5 | async-start | bytes 1048576 | tf_op jit(solution)/shard_map/all_to_all | solution.py:68
Sparse Core Ops, SparseCore 0:
  71.9 43.9 reduce-scatter.2
  118.1 42.8 reduce-scatter.4
where the time goes:
time: 186 us
  blocking collectives  58.4 us (31%)
  waiting for transfers between devices  49.8 us (27%)
  matrix products  26.5 us (14%)
  local copies, waits for them, and re-layouts  20.6 us (11%)
  between operations  13.6 us (7%)
  other arithmetic  9.89 us (5%)
  starting transfers between devices  7.2 us (4%)
    reduce_scatter x2, waiting for transfers between devices, project(): lax.psum_scatter(pieces.astype(jnp.bfloat16), 'tensor', scatter_dimension...  43.6 us
    all_to_all x1, blocking collectives, per_device(): lax.all_to_all(outgoing[:, 0:1], 'expert', split_axis=0, concat_axis=0, t...  30 us
    all_to_all x1, blocking collectives, per_device(): lax.all_to_all(outgoing[:, 1:2], 'expert', split_axis=0, concat_axis=0, t...  28.4 us
    dot_general x2, matrix products, project(): jnp.dot(hidden, weight_sets[which][2], preferred_element_type=jnp.float32)  20.6 us
    scatter x1, local copies, waits for them, and re-layouts, per_device(): jnp.zeros((experts * 2 * capacity, features), jnp.bfloat16).at[targets]  7.21 us
    all_to_all x2, starting transfers between devices, project(): lax.all_to_all(shares.astype(jnp.bfloat16), 'expert', split_axis=0, conca...  7.16 us
    all_to_all x2, waiting for transfers between devices, project(): lax.all_to_all(shares.astype(jnp.bfloat16), 'expert', split_axis=0, conca...  6.12 us
    dot_general x2, matrix products, project(): jnp.dot(flat_rows, weight_set[0], preferred_element_type=jnp.float32)  5.99 us
  transfers between devices with their start and end apart: 4, of which 3 were waited for; matrix products, arithmetic and copies ran while one was open for 8% of the time, Pallas kernels for 0%

commit v1 on v0

v1 whole, which is shorter than its diff:
```python
import functools

import jax
import jax.numpy as jnp
from jax import lax
from jax.experimental import pallas as pl
from jax.experimental.pallas import tpu as pltpu
from jax.sharding import PartitionSpec as P

LANES = 128
VMEM_LIMIT = 56 * 1024 * 1024
BF16 = jnp.bfloat16
F32 = jnp.float32


def prepare_kernel(experts, capacity, tok_ref, ids_ref, rw_ref, mod_ref, late_ref, early_ref, meta_ref):
    rows, width = tok_ref.shape
    values = tok_ref[...].astype(F32)
    mean = jnp.mean(values, axis=1, keepdims=True)
    centred = values - mean
    var = jnp.mean(centred * centred, axis=1, keepdims=True)
    inverse = 1.0 / jnp.sqrt(var + 1e-06)
    shift = mod_ref[:, 0:width]
    scale = mod_ref[:, width : 2 * width]
    modded = ((centred * inverse) * (1.0 + scale) + shift).astype(BF16)
    early_ref[...] = modded[:capacity]
    late_ref[...] = modded[capacity:]
    lane = lax.broadcasted_iota(jnp.int32, (rows, LANES), 1)
    quarter = lane // experts
    expert = lane - quarter * experts
    first = ids_ref[:, 0:1] == expert
    second = ids_ref[:, 1:2] == expert
    named = jnp.where(first | second, 1.0, 0.0).astype(BF16)
    row = lax.broadcasted_iota(jnp.int32, (rows, rows), 0)
    col = lax.broadcasted_iota(jnp.int32, (rows, rows), 1)
    below = jnp.where(col < row, 1.0, 0.0).astype(BF16)
    rank = jnp.dot(below, named, preferred_element_type=F32)
    weight = jnp.where(first, rw_ref[:, 0:1], 0.0) + jnp.where(second, rw_ref[:, 1:2], 0.0)
    high = weight.astype(BF16).astype(F32)
    part = jnp.where((quarter == 0) | (quarter == 2), high, weight - high)
    own = rank < float(capacity)
    wanted = ((quarter < 2) & own) | ((quarter >= 2) & (quarter < 4) & jnp.logical_not(own))
    meta_ref[...] = jnp.where(wanted, part, 0.0).astype(BF16)


def prepare(tokens, ids, weights, modulation, experts, capacity):
    rows, width = tokens.shape
    return pl.pallas_call(
        functools.partial(prepare_kernel, experts, capacity),
        out_shape=(
            jax.ShapeDtypeStruct((rows - capacity, width), BF16),
            jax.ShapeDtypeStruct((capacity, width), BF16),
            jax.ShapeDtypeStruct((rows, LANES), BF16),
        ),
        compiler_params=pltpu.CompilerParams(vmem_limit_bytes=24 * 1024 * 1024),
        cost_estimate=pl.CostEstimate(flops=12 * rows * width, bytes_accessed=4 * rows * width, transcendentals=0),
        name="prepare",
    )(tokens, ids, weights, modulation)


def ffn_kernel(experts, spans, spare_rows, blocks, shards, *refs):
    count = len(spans)
    partner_ref = refs[0]
    x_refs = refs[1 : 1 + count]
    meta_refs = refs[1 + count : 1 + 2 * count]
    rest = refs[1 + 2 * count :]
    home = rest[:3]
    spare = rest[3:6] if spare_rows else None
    rest = rest[6:] if spare_rows else rest[3:]
    out_refs = rest[:count]
    x_all, route, total = rest[count:]
    step = pl.program_id(0)
    steps = 2 * blocks if spare_rows else blocks
    width = x_all.shape[1]

    @pl.when(step == 0)
    def _():
        me = lax.axis_index("expert")
        source = jnp.int32(0)
        for e in range(experts):
            source = jnp.where(partner_ref[e] == me, e, source)
        start = 0
        for x_ref, meta_ref, (low, size) in zip(x_refs, meta_refs, spans):
            x_all[start : start + size, :] = x_ref[...]
            meta = meta_ref[low : low + size, :].astype(F32)
            lane = lax.broadcasted_iota(jnp.int32, (size, LANES), 1)
            mine = jnp.where((lane == me) | (lane == experts + me), meta, 0.0)
            route[0, start : start + size, :] = jnp.broadcast_to(
                jnp.sum(mine, axis=1, keepdims=True), (size, LANES)
            )
            theirs = jnp.where((lane == 2 * experts + source) | (lane == 3 * experts + source), meta, 0.0)
            route[1, start : start + size, :] = jnp.broadcast_to(
                jnp.sum(theirs, axis=1, keepdims=True), (size, LANES)
            )
            start += size

    def apply(which, height, weights):
        gate_w, up_w, down_w = weights
        values = x_all[:height, :]
        gate = jnp.dot(values, gate_w[0], preferred_element_type=F32)
        up = jnp.dot(values, up_w[0], preferred_element_type=F32)
        scaled = up * route[which, :height, 0:1]
        hidden = (gate / (1.0 + jnp.exp(-gate)) * scaled).astype(BF16)
        return jnp.dot(hidden, down_w[0], preferred_element_type=F32)

    height = x_all.shape[0]

    @pl.when(step == 0)
    def _():
        total[...] = apply(0, height, home)

    @pl.when((step > 0) & (step < blocks))
    def _():
        total[...] += apply(0, height, home)

    if spare_rows:

        @pl.when(step >= blocks)
        def _():
            total[:spare_rows, :] += apply(1, spare_rows, spare)

    @pl.when(step == steps - 1)
    def _():
        cols = width // shards
        start = 0
        for out_ref, (low, size) in zip(out_refs, spans):
            for shard in range(shards):
                out_ref[shard] = total[start : start + size, shard * cols : (shard + 1) * cols].astype(BF16)
            start += size


def ffn(name, xs, metas, spans, spare_rows, partner, home_set, spare_set, experts, shards, block=256):
    width = xs[0].shape[1]
    hidden = home_set[0].shape[2]
    block = min(block, hidden)
    blocks = hidden // block
    height = sum(size for _, size in spans)
    steps = 2 * blocks if spare_rows else blocks

    def weight_specs(at):
        return [
            pl.BlockSpec((1, width, block), lambda i: (0, 0, at(i))),
            pl.BlockSpec((1, width, block), lambda i: (0, 0, at(i))),
            pl.BlockSpec((1, block, width), lambda i: (0, at(i), 0)),
        ]

    whole = lambda a: pl.BlockSpec(a.shape, lambda i: (0,) * a.ndim)
    in_specs = [pl.BlockSpec(memory_space=pltpu.SMEM)] + [whole(a) for a in xs] + [whole(a) for a in metas]
    in_specs += weight_specs(lambda i: jnp.minimum(i, blocks - 1))
    operands = [partner, *xs, *metas, *home_set]
    if spare_rows:
        in_specs += weight_specs(lambda i: jnp.maximum(i - blocks, 0))
        operands += spare_set
    out_shape = [jax.ShapeDtypeStruct((shards, size, width // shards), BF16) for _, size in spans]
    work = height + spare_rows
    return pl.pallas_call(
        functools.partial(ffn_kernel, experts, spans, spare_rows, blocks, shards),
        out_shape=out_shape,
        grid=(steps,),
        in_specs=in_specs,
        out_specs=[pl.BlockSpec(s.shape, lambda i: (0, 0, 0)) for s in out_shape],
        scratch_shapes=[
            pltpu.VMEM((height, width), BF16),
            pltpu.VMEM((2, height, LANES), F32),
            pltpu.VMEM((height, width), F32),
        ],
        compiler_params=pltpu.CompilerParams(vmem_limit_bytes=VMEM_LIMIT),
        cost_estimate=pl.CostEstimate(
            flops=6 * work * width * hidden,
            bytes_accessed=6 * width * hidden * (2 if spare_rows else 1) + 4 * height * width,
            transcendentals=work * hidden,
        ),
        name=name,
    )(*operands)


def add(a, b):
    return (a.astype(F32) + b.astype(F32)).astype(BF16)


def per_device(
    tokens,
    route_ids,
    route_weights,
    modulation,
    partner,
    w_gate,
    w_up,
    w_down,
    spare_gate,
    spare_up,
    spare_down,
):
    experts = lax.axis_size("expert")
    shards = lax.axis_size("tensor")
    rows, width = tokens.shape
    capacity = 2 * rows // experts
    columns = width // shards
    chips = experts // 2
    shard = lax.axis_index("tensor")
    home_set = (w_gate, w_up, w_down)
    spare_set = (spare_gate, spare_up, spare_down)

    def core_swap(a):
        return lax.ppermute(a, "expert", [(e, e ^ 1) for e in range(experts)])

    def chip_hop(a, k):
        return lax.ppermute(a, "expert", [(e, (e + 2 * k) % experts) for e in range(experts)])

    def reduce_tensor(a):
        distance = 1
        while distance < shards:
            pairs = a.reshape((a.shape[0] // 2, 2) + a.shape[1:])
            bit = (shard // distance) % 2
            keep = lax.dynamic_index_in_dim(pairs, bit, 1, keepdims=False)
            give = lax.dynamic_index_in_dim(pairs, 1 - bit, 1, keepdims=False)
            got = lax.ppermute(give, "tensor", [(t, t ^ distance) for t in range(shards)])
            a = add(keep, got)
            distance *= 2
        return a[0]

    def deliver(a, k):
        got = []
        for j in range(shards):
            pairs = [
                (e * shards + t, ((e + 2 * k) % experts) * shards + (t + j) % shards)
                for e in range(experts)
                for t in range(shards)
            ]
            block = lax.dynamic_index_in_dim(a, (shard + j) % shards, 0, keepdims=False)
            got.append(lax.ppermute(block, ("expert", "tensor"), pairs))
        return got

    late, early, meta = prepare(tokens, route_ids, route_weights, modulation, experts, capacity)
    late_span = (capacity, rows - capacity)
    early_span = (0, capacity)

    hops = {}
    for k in range(1, chips):
        hops[k] = (chip_hop(meta, k), chip_hop(late, k), chip_hop(early, k))
    near = (core_swap(meta), core_swap(late), core_swap(early))
    call = functools.partial(
        ffn, partner=partner, home_set=home_set, spare_set=spare_set, experts=experts, shards=shards
    )

    late_keep, late_give, early_keep, early_give = call(
        "ffn_near",
        [late, near[1], early, near[2]],
        [meta, near[0], meta, near[0]],
        (late_span, late_span, early_span, early_span),
        2 * late_span[1],
    )
    early_sum = [reduce_tensor(add(early_keep, core_swap(early_give)))]
    late_sum = [reduce_tensor(add(late_keep, core_swap(late_give)))]

    for k in range(1, chips):
        meta_k, late_k, early_k = hops[k]
        meta_o, late_o, early_o = core_swap(meta_k), core_swap(late_k), core_swap(early_k)
        late_keep, late_give = call(
            "ffn_late", [late_k, late_o], [meta_k, meta_o], (late_span, late_span), 2 * late_span[1]
        )
        late_sum.append(chip_hop(reduce_tensor(add(late_keep, core_swap(late_give))), -k))
        early_keep, early_give = call("ffn_early", [early_k, early_o], [meta_k, meta_o], (early_span, early_span), 0)
        early_sum += deliver(add(early_keep, core_swap(early_give)), -k)

    def total(parts):
        result = parts[0].astype(F32)
        for part in parts[1:]:
            result = result + part.astype(F32)
        return result

    mixed = jnp.concatenate((total(early_sum), total(late_sum)), axis=0)
    own_cols = lax.dynamic_slice_in_dim(tokens, shard * columns, columns, 1).astype(F32)
    gate_cols = lax.dynamic_slice_in_dim(modulation[0], 2 * width + shard * columns, columns, 0)
    return (own_cols + gate_cols[None, :] * mixed).astype(BF16)


def solution(mesh):
    placed = (
        P(("groups", "expert"), None),
        P(("groups", "expert"), None),
        P(("groups", "expert"), None),
        P(("groups", "expert"), None),
        P(),
        P("expert", None, "tensor"),
        P("expert", None, "tensor"),
        P("expert", "tensor", None),
        P("expert", None, "tensor"),
        P("expert", None, "tensor"),
        P("expert", "tensor", None),
    )
    return jax.shard_map(
        per_device,
        mesh=mesh,
        in_specs=placed,
        out_specs=P(("groups", "expert"), "tensor"),
        check_vma=False,
    )
```

time: 186 us -> 112 us (0.60)
  blocking collectives: 58.4 us -> 0 us
  Pallas kernels: 0 us -> 46.2 us
  matrix products: 26.5 us -> 0 us
  waiting for transfers between devices: 49.8 us -> 29.6 us
  starting transfers between devices: 7.2 us -> 22.1 us
  between operations: 13.6 us -> 0.28 us
  local copies, waits for them, and re-layouts: 20.6 us -> 8.24 us
  other arithmetic: 9.89 us -> 4.92 us
    all_to_all x2 -> x0, blocking collectives: 58.4 us -> none  [the longest x1 30 us: per_device(): lax.all_to_all(outgoing[:, 0:1], 'expert', split_axis=0, concat_axis=0, t...]
    pallas_call x0 -> x4, Pallas kernels: none -> 46.2 us  [the longest x3 45.2 us: ffn(): pl.pallas_call(functools.partial(ffn_kernel, experts, spans, spare_rows,...]
    reduce_scatter x2 -> x0, waiting for transfers between devices: 43.6 us -> none  [project(): lax.psum_scatter(pieces.astype(jnp.bfloat16), 'tensor', scatter_dimension...]
    ppermute x0 -> x24, waiting for transfers between devices: none -> 29.6 us  [the longest x6 23.1 us: reduce_tensor(): lax.ppermute(give, 'tensor', [(t, t ^ distance) for t in range(shards)])]
    dot_general x4 -> x0, matrix products: 26.5 us -> none  [the longest x2 20.6 us: project(): jnp.dot(hidden, weight_sets[which][2], preferred_element_type=jnp.float32)]
    ppermute x0 -> x24, starting transfers between devices: none -> 22.1 us  [the longest x6 9.55 us: reduce_tensor(): lax.ppermute(give, 'tensor', [(t, t ^ distance) for t in range(shards)])]
    scatter x1 -> x0, local copies, waits for them, and re-layouts: 7.21 us -> none  [per_device(): jnp.zeros((experts * 2 * capacity, features), jnp.bfloat16).at[targets]]
    all_to_all x2 -> x0, starting transfers between devices: 7.16 us -> none  [project(): lax.all_to_all(shares.astype(jnp.bfloat16), 'expert', split_axis=0, conca...]
  transfers between devices with their start and end apart: 4 -> 24, of which waited for: 3 -> 7; matrix products, arithmetic and copies ran while one was open for 8% -> 4% of each run, Pallas kernels for 0% -> 41%
where the time goes in v1:
time: 112 us; the launch traced here: 111 us
  Pallas kernels  46.2 us (41%)
  waiting for transfers between devices  29.6 us (26%)
  starting transfers between devices  22.1 us (20%)
  local copies, waits for them, and re-layouts  8.24 us (7%)
  other arithmetic  4.92 us (4%)
    pallas_call x3, Pallas kernels, ffn(): pl.pallas_call(functools.partial(ffn_kernel, experts, spans, spare_rows,...  45.2 us
    ppermute x6, waiting for transfers between devices, reduce_tensor(): lax.ppermute(give, 'tensor', [(t, t ^ distance) for t in range(shards)])  23.1 us
    ppermute x6, starting transfers between devices, reduce_tensor(): lax.ppermute(give, 'tensor', [(t, t ^ distance) for t in range(shards)])  9.55 us
    unnamed x34, local copies, waits for them, and re-layouts  7.38 us
    ppermute x4, starting transfers between devices, chip_hop(): lax.ppermute(a, 'expert', [(e, (e + 2 * k) % experts) for e in range(expe...  6.24 us
    ppermute x4, waiting for transfers between devices, deliver(): got.append(lax.ppermute(block, ('expert', 'tensor'), pairs))  4.57 us
    ppermute x4, starting transfers between devices, deliver(): got.append(lax.ppermute(block, ('expert', 'tensor'), pairs))  3.42 us
    convert_element_type x7, other arithmetic, add(): return (a.astype(F32) + b.astype(F32)).astype(BF16)  2.98 us
  transfers between devices with their start and end apart: 24, of which 7 were waited for; matrix products, arithmetic and copies ran while one was open for 4% of the time, Pallas kernels for 41%

profile of v1, /device:TPU:0, one launch (start us, length us, event | category | flops | bytes accessed | tf_op | source)
XLA Modules:
  0.0 111.3 jit_solution(9291130316493559794)
XLA Ops:
  0.0 0.8 copy.12.ids_ref
  0.8 0.8 copy.13.rw_ref
  1.6 0.0 copy-start
  1.6 1.2 %copy-done = bf16[256,2048]{1,0:T(8,128)(2,1)S(1)} copy-done((bf16[256,2048]{1,0:T(8,128)(2,1)S(1)}, bf16[256,2048]{1,0:T(8,128)(2,1)}, u32[]{:S(2)}) %copy-start) | copy-done | bytes 1048600
  2.9 0.7 copy-done.1
  3.6 1.0 prepare.1
  4.7 0.0 copy-start.4
  4.7 0.6 collective-permute-start
  5.2 0.1 collective-permute-start.1
  5.3 0.4 collective-permute-start.2
  5.7 2.6 %collective-permute-start.6 = (bf16[128,2048]{1,0:T(8,128)(2,1)S(1)}, bf16[128,2048]{1,0:T(8,128)(2,1)S(1)}, u32[]{:S(2)}, u32[]{:S(2)}) collective-permute-start(bf16[128,2048]{1,0:T(8,128)(2,1)S(1)} %get-tuple-element.17.refs_3_), channel_id=1, source_target_pairs={{0,8},{4,12},{8,0},{12,4},{1,9},{5,13},{9,1},{13,5},{2,10},{6,14},... | collective-permute-start | bytes 1572872 | tf_op jit(solution)/shard_map/ppermute | solution.py:208
  8.3 0.0 collective-permute-start.18
  8.3 0.0 collective-permute-done.1.refs_4_
  8.4 0.6 copy-done.15
  9.0 0.2 copy-done.13
  9.2 0.8 copy-done.14
  10.0 19.8 %ffn_near.1 = (bf16[4,128,512]{2,1,0:T(8,128)(2,1)}, bf16[4,128,512]{2,1,0:T(8,128)(2,1)}, bf16[4,128,512]{2,1,0:T(8,128)(2,1)}, bf16[4,128,512]{2,1,0:T(8,128)(2,1)}) custom-call(s32[4]{0:T(128)} %refs_0_.5, bf16[128,2048]{1,0:T(8,128)(2,1)} %copy-done.2, bf16[128,2048]{1,0:T(8,128)(2,1)} %copy-done.13, bf16[128,2048]{1,0:T(8,128)(2,1)} %copy-done.3, ...), custom_call_target="tpu_custom_call" | custom-call | flops 9663676416 | bytes 29360128 | tf_op jit(solution)/shard_map/ffn_near/pallas_call | solution.py:156
  29.7 0.2 collective-permute-start.3
  29.9 0.0 collective-permute-done.6.refs_1_
  29.9 0.4 collective-permute-start.7
  30.3 2.1 %collective-permute-start.8 = (bf16[256,128]{1,0:T(8,128)(2,1)}, bf16[256,128]{1,0:T(8,128)(2,1)S(1)}, u32[]{:S(2)}, u32[]{:S(2)}) collective-permute-start(bf16[256,128]{1,0:T(8,128)(2,1)} %copy-done.4), channel_id=1, source_target_pairs={{0,8},{4,12},{8,0},{12,4},{1,9},{5,13},{9,1},{13,5},{2,10},{6,14},... | collective-permute-start | bytes 196616 | tf_op jit(solution)/shard_map/ppermute | solution.py:208
  32.4 0.7 constant_dynamic-slice_fusion.3
  33.1 1.9 %collective-permute-done.8.refs_3_ = bf16[256,128]{1,0:T(8,128)(2,1)S(1)} collective-permute-done((bf16[256,128]{1,0:T(8,128)(2,1)}, bf16[256,128]{1,0:T(8,128)(2,1)S(1)}, u32[]{:S(2)}, u32[]{:S(2)}) %collective-permute-start.8) | collective-permute-done | bytes 65568 | tf_op jit(solution)/shard_map/ppermute | solution.py:208
  35.0 0.5 collective-permute-start.15
  35.6 0.0 collective-permute-done.18.refs_1_
  35.6 0.1 collective-permute-start.19
  35.6 0.0 collective-permute-done.3
  35.6 1.3 %add_convert_fusion.3 = bf16[4,128,512]{2,1,0:T(8,128)(2,1)S(1)} fusion(bf16[4,128,512]{2,1,0:T(8,128)(2,1)S(1)} %collective-permute-done.3, bf16[4,128,512]{2,1,0:T(8,128)(2,1)} %get-tuple-element.19), kind=kLoop, calls=%fused_computation.3 | loop fusion | flops 1048576 | bytes 1572864 | tf_op jit(solution)/shard_map/convert_element_type | solution.py:178
  37.0 2.0 %collective-permute-start.4 = (bf16[2,128,512]{2,1,0:T(8,128)(2,1)S(1)}, bf16[2,128,512]{2,1,0:T(8,128)(2,1)S(1)}, u32[]{:S(2)}, u32[]{:S(2)}) collective-permute-start(bf16[2,128,512]{2,1,0:T(8,128)(2,1)S(1)} %dynamic-slice_bitcast_fusion.2), channel_id=1, source_target_pairs={{0,1},{1,0},{2,3},{3,2},{4,5},{5,4},{6,7},{7,6},{8,9},{9,8},{10,11... | collective-permute-start | bytes 786440 | tf_op jit(solution)/shard_map/ppermute | solution.py:217
  39.0 0.0 collective-permute-done.9.refs_4_
  39.0 0.6 copy-done.12
  39.6 0.8 copy-done.10
  40.4 9.1 %ffn_early.1 = (bf16[4,128,512]{2,1,0:T(8,128)(2,1)}, bf16[4,128,512]{2,1,0:T(8,128)(2,1)}) custom-call(s32[4]{0:T(128)} %refs_0_.5, bf16[128,2048]{1,0:T(8,128)(2,1)} %copy-done.9, bf16[128,2048]{1,0:T(8,128)(2,1)} %copy-done.10, bf16[256,128]{1,0:T(8,128)(2,1)} %copy-done.11, bf16[256,128]{1,0:T(8,128)(2,1)} %copy-done.12, bf16[1,2048,1024]{2,1,0:T(8,128)(2,1)} %refs_5_.3, ...), custom_call_target="tpu_custom_call" | custom-call | flops 3221225472 | bytes 14680064 | tf_op jit(solution)/shard_map/ffn_early/pallas_call | solution.py:156
  49.6 0.1 collective-permute-start.10
  49.7 0.0 collective-permute-done.19.refs_2_
  49.7 0.8 copy-done.8
  50.5 16.3 %ffn_late.1 = (bf16[4,128,512]{2,1,0:T(8,128)(2,1)}, bf16[4,128,512]{2,1,0:T(8,128)(2,1)}) custom-call(s32[4]{0:T(128)} %refs_0_.5, bf16[128,2048]{1,0:T(8,128)(2,1)} %copy-done.5, bf16[128,2048]{1,0:T(8,128)(2,1)} %copy-done.8, bf16[256,128]{1,0:T(8,128)(2,1)} %copy-done.11, bf16[256,128]{1,0:T(8,128)(2,1)} %copy-done.12, bf16[1,2048,1024]{2,1,0:T(8,128)(2,1)} %refs_5_.3, ...), custom_call_target="tpu_custom_call" | custom-call | flops 6442450944 | bytes 27262976 | tf_op jit(solution)/shard_map/ffn_late/pallas_call | solution.py:156
  66.7 0.5 collective-permute-start.20
  67.3 0.0 collective-permute-done.15
  67.3 0.1 add_convert_fusion.1
  67.5 0.1 collective-permute-start.16
  67.6 0.1 fusion.4
  67.7 3.1 %collective-permute-start.5 = (bf16[1,128,512]{2,1,0:T(8,128)(2,1)S(1)}, bf16[1,128,512]{2,1,0:T(8,128)(2,1)S(1)}, u32[]{:S(2)}, u32[]{:S(2)}) collective-permute-start(bf16[1,128,512]{2,1,0:T(8,128)(2,1)S(1)} %constant_dynamic-slice_fusion.2), channel_id=1, source_target_pairs={{0,2},{1,3},{2,0},{3,1},{4,6},{5,7},{6,4},{7,5},{8,10},{9,11},{10,... | collective-permute-start | bytes 393224 | tf_op jit(solution)/shard_map/ppermute | solution.py:217
  70.8 0.0 collective-permute-done.20
  70.8 1.2 %add_convert_fusion = bf16[4,128,512]{2,1,0:T(8,128)(2,1)S(1)} fusion(bf16[4,128,512]{2,1,0:T(8,128)(2,1)S(1)} %collective-permute-done.20, bf16[4,128,512]{2,1,0:T(8,128)(2,1)} %get-tuple-element.25), kind=kLoop, calls=%fused_computation | loop fusion | flops 1048576 | bytes 1572864 | tf_op jit(solution)/shard_map/convert_element_type | solution.py:178
  72.0 1.6 %collective-permute-start.21 = (bf16[2,128,512]{2,1,0:T(8,128)(2,1)S(1)}, bf16[2,128,512]{2,1,0:T(8,128)(2,1)S(1)}, u32[]{:S(2)}, u32[]{:S(2)}) collective-permute-start(bf16[2,128,512]{2,1,0:T(8,128)(2,1)S(1)} %dynamic-slice_bitcast_fusion), channel_id=1, source_target_pairs={{0,1},{1,0},{2,3},{3,2},{4,5},{5,4},{6,7},{7,6},{8,9},{9,8},{10,11... | collective-permute-start | bytes 786440 | tf_op jit(solution)/shard_map/ppermute | solution.py:217
  73.6 5.9 %collective-permute-done.16 = bf16[2,128,512]{2,1,0:T(8,128)(2,1)S(1)} collective-permute-done((bf16[2,128,512]{2,1,0:T(8,128)(2,1)S(1)}, bf16[2,128,512]{2,1,0:T(8,128)(2,1)S(1)}, u32[]{:S(2)}, u32[]{:S(2)}) %collective-permute-start.16) | collective-permute-done | bytes 262176 | tf_op jit(solution)/shard_map/ppermute | solution.py:217
  79.5 0.1 fusion.3
  79.6 4.6 %collective-permute-done.21 = bf16[2,128,512]{2,1,0:T(8,128)(2,1)S(1)} collective-permute-done((bf16[2,128,512]{2,1,0:T(8,128)(2,1)S(1)}, bf16[2,128,512]{2,1,0:T(8,128)(2,1)S(1)}, u32[]{:S(2)}, u32[]{:S(2)}) %collective-permute-start.21) | collective-permute-done | bytes 262176 | tf_op jit(solution)/shard_map/ppermute | solution.py:217
  84.2 0.1 fusion.2
  84.3 2.6 %collective-permute-start.22 = (bf16[1,128,512]{2,1,0:T(8,128)(2,1)S(1)}, bf16[1,128,512]{2,1,0:T(8,128)(2,1)S(1)}, u32[]{:S(2)}, u32[]{:S(2)}) collective-permute-start(bf16[1,128,512]{2,1,0:T(8,128)(2,1)S(1)} %constant_dynamic-slice_fusion), channel_id=1, source_target_pairs={{0,2},{1,3},{2,0},{3,1},{4,6},{5,7},{6,4},{7,5},{8,10},{9,11},{10,... | collective-permute-start | bytes 393224 | tf_op jit(solution)/shard_map/ppermute | solution.py:217
  87.0 0.1 add_convert_fusion.2
  87.2 1.6 %collective-permute-start.11 = (bf16[128,512]{1,0:T(8,128)(2,1)S(1)}, bf16[128,512]{1,0:T(8,128)(2,1)S(1)}, u32[]{:S(2)}, u32[]{:S(2)}) collective-permute-start(bf16[128,512]{1,0:T(8,128)(2,1)S(1)} %get-tuple-element.27), channel_id=1, source_target_pairs={{0,8},{1,9},{2,10},{3,11},{4,12},{5,13},{6,14},{7,15},{8,0},{9,1},... | collective-permute-start | bytes 393224 | tf_op jit(solution)/shard_map/ppermute | solution.py:231
  88.7 0.4 collective-permute-start.12
  89.2 1.3 %collective-permute-start.13 = (bf16[128,512]{1,0:T(8,128)(2,1)S(1)}, bf16[128,512]{1,0:T(8,128)(2,1)S(1)}, u32[]{:S(2)}, u32[]{:S(2)}) collective-permute-start(bf16[128,512]{1,0:T(8,128)(2,1)S(1)} %get-tuple-element.29), channel_id=1, source_target_pairs={{0,10},{1,11},{2,8},{3,9},{4,14},{5,15},{6,12},{7,13},{8,2},{9,3},... | collective-permute-start | bytes 393224 | tf_op jit(solution)/shard_map/ppermute | solution.py:231
  90.4 8.0 %collective-permute-done.22 = bf16[1,128,512]{2,1,0:T(8,128)(2,1)S(1)} collective-permute-done((bf16[1,128,512]{2,1,0:T(8,128)(2,1)S(1)}, bf16[1,128,512]{2,1,0:T(8,128)(2,1)S(1)}, u32[]{:S(2)}, u32[]{:S(2)}) %collective-permute-start.22) | collective-permute-done | bytes 131104 | tf_op jit(solution)/shard_map/ppermute | solution.py:217
  98.4 0.2 collective-permute-start.14
  98.6 0.1 collective-permute-start.17
  98.7 1.5 %collective-permute-start.23 = (bf16[128,512]{1,0:T(8,128)(2,1)S(1)}, bf16[128,512]{1,0:T(8,128)(2,1)S(1)}, u32[]{:S(2)}, u32[]{:S(2)}) collective-permute-start(bf16[128,512]{1,0:T(8,128)(2,1)S(1)} %fusion.10), channel_id=1, source_target_pairs={{0,8},{4,12},{8,0},{12,4},{1,9},{5,13},{9,1},{13,5},{2,10},{6,14},... | collective-permute-start | bytes 393224 | tf_op jit(solution)/shard_map/ppermute | solution.py:208
  100.3 2.0 %collective-permute-done.13 = bf16[128,512]{1,0:T(8,128)(2,1)S(1)} collective-permute-done((bf16[128,512]{1,0:T(8,128)(2,1)S(1)}, bf16[128,512]{1,0:T(8,128)(2,1)S(1)}, u32[]{:S(2)}, u32[]{:S(2)}) %collective-permute-start.13) | collective-permute-done | bytes 131104 | tf_op jit(solution)/shard_map/ppermute | solution.py:231
  102.3 2.5 %collective-permute-done.14 = bf16[128,512]{1,0:T(8,128)(2,1)S(1)} collective-permute-done((bf16[128,512]{1,0:T(8,128)(2,1)S(1)}, bf16[128,512]{1,0:T(8,128)(2,1)S(1)}, u32[]{:S(2)}, u32[]{:S(2)}) %collective-permute-start.14) | collective-permute-done | bytes 131104 | tf_op jit(solution)/shard_map/ppermute | solution.py:231
  104.8 0.1 fusion.7
  104.9 4.6 %collective-permute-done.17 = bf16[1,128,512]{2,1,0:T(8,128)(2,1)S(1)} collective-permute-done((bf16[1,128,512]{2,1,0:T(8,128)(2,1)S(1)}, bf16[1,128,512]{2,1,0:T(8,128)(2,1)S(1)}, u32[]{:S(2)}, u32[]{:S(2)}) %collective-permute-start.17) | collective-permute-done | bytes 131104 | tf_op jit(solution)/shard_map/ppermute | solution.py:217
  109.5 1.7 %fusion.1 = bf16[256,512]{1,0:T(8,128)(2,1)} fusion(f32[128,512]{1,0:T(8,128)S(1)} %convert_add_fusion.3, f32[128,512]{1,0:T(8,128)S(1)} %fusion.7, f32[512]{0:T(512)S(1)} %bitcast.51, bf16[256,2048]{1,0:T(8,128)(2,1)} %tok_ref.1, s32[]{:T(128)S(6)} %select_n.85), kind=kLoop, calls=%fused_computation.6 | loop fusion | flops 655360 | bytes 1050628 | tf_op jit(solution)/shard_map/convert_element_type | solution.py:275
  (41 shorter events, 0.3 us)
Async XLA Ops:
  1.6 1.2 %copy-start = (bf16[256,2048]{1,0:T(8,128)(2,1)S(1)}, bf16[256,2048]{1,0:T(8,128)(2,1)}, u32[]{:S(2)}) copy-start(bf16[256,2048]{1,0:T(8,128)(2,1)} %tok_ref.1) | copy-start | bytes 3145732
  2.9 0.7 copy-start.1
  4.6 3.7 %copy-start.2 = (bf16[128,2048]{1,0:T(8,128)(2,1)}, bf16[128,2048]{1,0:T(8,128)(2,1)S(1)}, u32[]{:S(2)}) copy-start(bf16[128,2048]{1,0:T(8,128)(2,1)S(1)} %get-tuple-element.16.refs_1_) | copy-start | bytes 1572868
  4.6 3.7 %copy-start.3 = (bf16[128,2048]{1,0:T(8,128)(2,1)}, bf16[128,2048]{1,0:T(8,128)(2,1)S(1)}, u32[]{:S(2)}) copy-start(bf16[128,2048]{1,0:T(8,128)(2,1)S(1)} %get-tuple-element.17.refs_3_) | copy-start | bytes 1572868
  4.7 3.7 %copy-start.4 = (bf16[256,128]{1,0:T(8,128)(2,1)}, bf16[256,128]{1,0:T(8,128)(2,1)S(1)}, u32[]{:S(2)}) copy-start(bf16[256,128]{1,0:T(8,128)(2,1)S(1)} %get-tuple-element.18.refs_5_.refs_7_) | copy-start | bytes 196612
  4.7 3.7 %collective-permute-start = (bf16[128,2048]{1,0:T(8,128)(2,1)S(1)}, bf16[128,2048]{1,0:T(8,128)(2,1)S(1)}, u32[]{:S(2)}, u32[]{:S(2)}) collective-permute-start(bf16[128,2048]{1,0:T(8,128)(2,1)S(1)} %get-tuple-element.16.refs_1_), channel_id=1, source_target_pairs={{0,4},{4,0},{8,12},{12,8},{1,5},{5,1},{9,13},{13,9},{2,6},{6,2},{1... | collective-permute-start | bytes 1572872 | tf_op jit(solution)/shard_map/ppermute | solution.py:205
  5.2 3.1 %collective-permute-start.1 = (bf16[128,2048]{1,0:T(8,128)(2,1)S(1)}, bf16[128,2048]{1,0:T(8,128)(2,1)S(1)}, u32[]{:S(2)}, u32[]{:S(2)}) collective-permute-start(bf16[128,2048]{1,0:T(8,128)(2,1)S(1)} %get-tuple-element.17.refs_3_), channel_id=1, source_target_pairs={{0,4},{4,0},{8,12},{12,8},{1,5},{5,1},{9,13},{13,9},{2,6},{6,2},{1... | collective-permute-start | bytes 1572872 | tf_op jit(solution)/shard_map/ppermute | solution.py:205
  5.3 3.0 %collective-permute-start.2 = (bf16[256,128]{1,0:T(8,128)(2,1)S(1)}, bf16[256,128]{1,0:T(8,128)(2,1)S(1)}, u32[]{:S(2)}, u32[]{:S(2)}) collective-permute-start(bf16[256,128]{1,0:T(8,128)(2,1)S(1)} %get-tuple-element.18.refs_5_.refs_7_), channel_id=1, source_target_pairs={{0,4},{4,0},{8,12},{12,8},{1,5},{5,1},{9,13},{13,9},{2,6},{6,2},{1... | collective-permute-start | bytes 196616 | tf_op jit(solution)/shard_map/ppermute | solution.py:205
  5.7 24.2 %collective-permute-start.6 = (bf16[128,2048]{1,0:T(8,128)(2,1)S(1)}, bf16[128,2048]{1,0:T(8,128)(2,1)S(1)}, u32[]{:S(2)}, u32[]{:S(2)}) collective-permute-start(bf16[128,2048]{1,0:T(8,128)(2,1)S(1)} %get-tuple-element.17.refs_3_), channel_id=1, source_target_pairs={{0,8},{4,12},{8,0},{12,4},{1,9},{5,13},{9,1},{13,5},{2,10},{6,14},... | collective-permute-start | bytes 1572872 | tf_op jit(solution)/shard_map/ppermute | solution.py:208
  8.3 27.3 %collective-permute-start.18 = (bf16[128,2048]{1,0:T(8,128)(2,1)S(1)}, bf16[128,2048]{1,0:T(8,128)(2,1)S(1)}, u32[]{:S(2)}, u32[]{:S(2)}) collective-permute-start(bf16[128,2048]{1,0:T(8,128)(2,1)S(1)} %get-tuple-element.16.refs_1_), channel_id=1, source_target_pairs={{0,8},{4,12},{8,0},{12,4},{1,9},{5,13},{9,1},{13,5},{2,10},{6,14},... | collective-permute-start | bytes 1572872 | tf_op jit(solution)/shard_map/ppermute | solution.py:208
  8.3 0.6 copy-start.15
  8.3 0.8 copy-start.13
  9.2 0.8 copy-start.14
  29.7 5.9 %collective-permute-start.3 = (bf16[4,128,512]{2,1,0:T(8,128)(2,1)}, bf16[4,128,512]{2,1,0:T(8,128)(2,1)S(1)}, u32[]{:S(2)}, u32[]{:S(2)}) collective-permute-start(bf16[4,128,512]{2,1,0:T(8,128)(2,1)} %get-tuple-element.20), channel_id=1, source_target_pairs={{0,4},{4,0},{8,12},{12,8},{1,5},{5,1},{9,13},{13,9},{2,6},{6,2},{1... | collective-permute-start | bytes 1572872 | tf_op jit(solution)/shard_map/ppermute | solution.py:205
  29.9 9.1 %copy-start.9 = (bf16[128,2048]{1,0:T(8,128)(2,1)}, bf16[128,2048]{1,0:T(8,128)(2,1)S(1)}, u32[]{:S(2)}) copy-start(bf16[128,2048]{1,0:T(8,128)(2,1)S(1)} %collective-permute-done.6.refs_1_) | copy-start | bytes 1572868
  29.9 9.1 %collective-permute-start.7 = (bf16[128,2048]{1,0:T(8,128)(2,1)S(1)}, bf16[128,2048]{1,0:T(8,128)(2,1)S(1)}, u32[]{:S(2)}, u32[]{:S(2)}) collective-permute-start(bf16[128,2048]{1,0:T(8,128)(2,1)S(1)} %collective-permute-done.6.refs_1_), channel_id=1, source_target_pairs={{0,4},{4,0},{8,12},{12,8},{1,5},{5,1},{9,13},{13,9},{2,6},{6,2},{1... | collective-permute-start | bytes 1572872 | tf_op jit(solution)/shard_map/ppermute | solution.py:205
  30.3 4.7 %collective-permute-start.8 = (bf16[256,128]{1,0:T(8,128)(2,1)}, bf16[256,128]{1,0:T(8,128)(2,1)S(1)}, u32[]{:S(2)}, u32[]{:S(2)}) collective-permute-start(bf16[256,128]{1,0:T(8,128)(2,1)} %copy-done.4), channel_id=1, source_target_pairs={{0,8},{4,12},{8,0},{12,4},{1,9},{5,13},{9,1},{13,5},{2,10},{6,14},... | collective-permute-start | bytes 196616 | tf_op jit(solution)/shard_map/ppermute | solution.py:208
  35.0 4.0 %copy-start.11 = (bf16[256,128]{1,0:T(8,128)(2,1)}, bf16[256,128]{1,0:T(8,128)(2,1)S(1)}, u32[]{:S(2)}) copy-start(bf16[256,128]{1,0:T(8,128)(2,1)S(1)} %collective-permute-done.8.refs_3_) | copy-start | bytes 196612
  35.0 4.0 %collective-permute-start.9 = (bf16[256,128]{1,0:T(8,128)(2,1)S(1)}, bf16[256,128]{1,0:T(8,128)(2,1)S(1)}, u32[]{:S(2)}, u32[]{:S(2)}) collective-permute-start(bf16[256,128]{1,0:T(8,128)(2,1)S(1)} %collective-permute-done.8.refs_3_), channel_id=1, source_target_pairs={{0,4},{4,0},{8,12},{12,8},{1,5},{5,1},{9,13},{13,9},{2,6},{6,2},{1... | collective-permute-start | bytes 196616 | tf_op jit(solution)/shard_map/ppermute | solution.py:205
  35.0 32.2 %collective-permute-start.15 = (bf16[4,128,512]{2,1,0:T(8,128)(2,1)}, bf16[4,128,512]{2,1,0:T(8,128)(2,1)S(1)}, u32[]{:S(2)}, u32[]{:S(2)}) collective-permute-start(bf16[4,128,512]{2,1,0:T(8,128)(2,1)} %get-tuple-element.24), channel_id=1, source_target_pairs={{0,4},{4,0},{8,12},{12,8},{1,5},{5,1},{9,13},{13,9},{2,6},{6,2},{1... | collective-permute-start | bytes 1572872 | tf_op jit(solution)/shard_map/ppermute | solution.py:205
  35.6 14.0 %copy-start.5 = (bf16[128,2048]{1,0:T(8,128)(2,1)}, bf16[128,2048]{1,0:T(8,128)(2,1)S(1)}, u32[]{:S(2)}) copy-start(bf16[128,2048]{1,0:T(8,128)(2,1)S(1)} %collective-permute-done.18.refs_1_) | copy-start | bytes 1572868
  35.6 14.1 %collective-permute-start.19 = (bf16[128,2048]{1,0:T(8,128)(2,1)S(1)}, bf16[128,2048]{1,0:T(8,128)(2,1)S(1)}, u32[]{:S(2)}, u32[]{:S(2)}) collective-permute-start(bf16[128,2048]{1,0:T(8,128)(2,1)S(1)} %collective-permute-done.18.refs_1_), channel_id=1, source_target_pairs={{0,4},{4,0},{8,12},{12,8},{1,5},{5,1},{9,13},{13,9},{2,6},{6,2},{1... | collective-permute-start | bytes 1572872 | tf_op jit(solution)/shard_map/ppermute | solution.py:205
  37.0 30.6 %collective-permute-start.4 = (bf16[2,128,512]{2,1,0:T(8,128)(2,1)S(1)}, bf16[2,128,512]{2,1,0:T(8,128)(2,1)S(1)}, u32[]{:S(2)}, u32[]{:S(2)}) collective-permute-start(bf16[2,128,512]{2,1,0:T(8,128)(2,1)S(1)} %dynamic-slice_bitcast_fusion.2), channel_id=1, source_target_pairs={{0,1},{1,0},{2,3},{3,2},{4,5},{5,4},{6,7},{7,6},{8,9},{9,8},{10,11... | collective-permute-start | bytes 786440 | tf_op jit(solution)/shard_map/ppermute | solution.py:217
  39.0 0.6 copy-start.12
  39.6 0.8 copy-start.10
  49.6 17.7 %copy-start.6 = (bf16[4,128,512]{2,1,0:T(8,128)(2,1)S(1)}, bf16[4,128,512]{2,1,0:T(8,128)(2,1)}, u32[]{:S(2)}) copy-start(bf16[4,128,512]{2,1,0:T(8,128)(2,1)} %get-tuple-element.23) | copy-start | bytes 1572868
  49.6 37.4 %collective-permute-start.10 = (bf16[4,128,512]{2,1,0:T(8,128)(2,1)}, bf16[4,128,512]{2,1,0:T(8,128)(2,1)S(1)}, u32[]{:S(2)}, u32[]{:S(2)}) collective-permute-start(bf16[4,128,512]{2,1,0:T(8,128)(2,1)} %get-tuple-element.22), channel_id=1, source_target_pairs={{0,4},{4,0},{8,12},{12,8},{1,5},{5,1},{9,13},{13,9},{2,6},{6,2},{1... | collective-permute-start | bytes 1572872 | tf_op jit(solution)/shard_map/ppermute | solution.py:205
  49.7 0.8 copy-start.8
  66.7 20.2 %copy-start.7 = (bf16[4,128,512]{2,1,0:T(8,128)(2,1)S(1)}, bf16[4,128,512]{2,1,0:T(8,128)(2,1)}, u32[]{:S(2)}) copy-start(bf16[4,128,512]{2,1,0:T(8,128)(2,1)} %get-tuple-element.21) | copy-start | bytes 1572868
  66.7 4.0 %collective-permute-start.20 = (bf16[4,128,512]{2,1,0:T(8,128)(2,1)}, bf16[4,128,512]{2,1,0:T(8,128)(2,1)S(1)}, u32[]{:S(2)}, u32[]{:S(2)}) collective-permute-start(bf16[4,128,512]{2,1,0:T(8,128)(2,1)} %get-tuple-element.26), channel_id=1, source_target_pairs={{0,4},{4,0},{8,12},{12,8},{1,5},{5,1},{9,13},{13,9},{2,6},{6,2},{1... | collective-permute-start | bytes 1572872 | tf_op jit(solution)/shard_map/ppermute | solution.py:205
  67.5 12.1 %collective-permute-start.16 = (bf16[2,128,512]{2,1,0:T(8,128)(2,1)S(1)}, bf16[2,128,512]{2,1,0:T(8,128)(2,1)S(1)}, u32[]{:S(2)}, u32[]{:S(2)}) collective-permute-start(bf16[2,128,512]{2,1,0:T(8,128)(2,1)S(1)} %dynamic-slice_bitcast_fusion.1), channel_id=1, source_target_pairs={{0,1},{1,0},{2,3},{3,2},{4,5},{5,4},{6,7},{7,6},{8,9},{9,8},{10,11... | collective-permute-start | bytes 786440 | tf_op jit(solution)/shard_map/ppermute | solution.py:217
  67.7 30.9 %collective-permute-start.5 = (bf16[1,128,512]{2,1,0:T(8,128)(2,1)S(1)}, bf16[1,128,512]{2,1,0:T(8,128)(2,1)S(1)}, u32[]{:S(2)}, u32[]{:S(2)}) collective-permute-start(bf16[1,128,512]{2,1,0:T(8,128)(2,1)S(1)} %constant_dynamic-slice_fusion.2), channel_id=1, source_target_pairs={{0,2},{1,3},{2,0},{3,1},{4,6},{5,7},{6,4},{7,5},{8,10},{9,11},{10,... | collective-permute-start | bytes 393224 | tf_op jit(solution)/shard_map/ppermute | solution.py:217
  72.0 12.2 %collective-permute-start.21 = (bf16[2,128,512]{2,1,0:T(8,128)(2,1)S(1)}, bf16[2,128,512]{2,1,0:T(8,128)(2,1)S(1)}, u32[]{:S(2)}, u32[]{:S(2)}) collective-permute-start(bf16[2,128,512]{2,1,0:T(8,128)(2,1)S(1)} %dynamic-slice_bitcast_fusion), channel_id=1, source_target_pairs={{0,1},{1,0},{2,3},{3,2},{4,5},{5,4},{6,7},{7,6},{8,9},{9,8},{10,11... | collective-permute-start | bytes 786440 | tf_op jit(solution)/shard_map/ppermute | solution.py:217
  84.3 14.1 %collective-permute-start.22 = (bf16[1,128,512]{2,1,0:T(8,128)(2,1)S(1)}, bf16[1,128,512]{2,1,0:T(8,128)(2,1)S(1)}, u32[]{:S(2)}, u32[]{:S(2)}) collective-permute-start(bf16[1,128,512]{2,1,0:T(8,128)(2,1)S(1)} %constant_dynamic-slice_fusion), channel_id=1, source_target_pairs={{0,2},{1,3},{2,0},{3,1},{4,6},{5,7},{6,4},{7,5},{8,10},{9,11},{10,... | collective-permute-start | bytes 393224 | tf_op jit(solution)/shard_map/ppermute | solution.py:217
  87.2 11.6 %collective-permute-start.11 = (bf16[128,512]{1,0:T(8,128)(2,1)S(1)}, bf16[128,512]{1,0:T(8,128)(2,1)S(1)}, u32[]{:S(2)}, u32[]{:S(2)}) collective-permute-start(bf16[128,512]{1,0:T(8,128)(2,1)S(1)} %get-tuple-element.27), channel_id=1, source_target_pairs={{0,8},{1,9},{2,10},{3,11},{4,12},{5,13},{6,14},{7,15},{8,0},{9,1},... | collective-permute-start | bytes 393224 | tf_op jit(solution)/shard_map/ppermute | solution.py:231
  88.7 11.5 %collective-permute-start.12 = (bf16[128,512]{1,0:T(8,128)(2,1)S(1)}, bf16[128,512]{1,0:T(8,128)(2,1)S(1)}, u32[]{:S(2)}, u32[]{:S(2)}) collective-permute-start(bf16[128,512]{1,0:T(8,128)(2,1)S(1)} %get-tuple-element.30), channel_id=1, source_target_pairs={{0,9},{1,10},{2,11},{3,8},{4,13},{5,14},{6,15},{7,12},{8,1},{9,2},... | collective-permute-start | bytes 393224 | tf_op jit(solution)/shard_map/ppermute | solution.py:231
  89.2 13.1 %collective-permute-start.13 = (bf16[128,512]{1,0:T(8,128)(2,1)S(1)}, bf16[128,512]{1,0:T(8,128)(2,1)S(1)}, u32[]{:S(2)}, u32[]{:S(2)}) collective-permute-start(bf16[128,512]{1,0:T(8,128)(2,1)S(1)} %get-tuple-element.29), channel_id=1, source_target_pairs={{0,10},{1,11},{2,8},{3,9},{4,14},{5,15},{6,12},{7,13},{8,2},{9,3},... | collective-permute-start | bytes 393224 | tf_op jit(solution)/shard_map/ppermute | solution.py:231
  98.4 6.4 %collective-permute-start.14 = (bf16[128,512]{1,0:T(8,128)(2,1)S(1)}, bf16[128,512]{1,0:T(8,128)(2,1)S(1)}, u32[]{:S(2)}, u32[]{:S(2)}) collective-permute-start(bf16[128,512]{1,0:T(8,128)(2,1)S(1)} %get-tuple-element.28), channel_id=1, source_target_pairs={{0,11},{1,8},{2,9},{3,10},{4,15},{5,12},{6,13},{7,14},{8,3},{9,0},... | collective-permute-start | bytes 393224 | tf_op jit(solution)/shard_map/ppermute | solution.py:231
  98.6 10.9 %collective-permute-start.17 = (bf16[1,128,512]{2,1,0:T(8,128)(2,1)S(1)}, bf16[1,128,512]{2,1,0:T(8,128)(2,1)S(1)}, u32[]{:S(2)}, u32[]{:S(2)}) collective-permute-start(bf16[1,128,512]{2,1,0:T(8,128)(2,1)S(1)} %constant_dynamic-slice_fusion.1), channel_id=1, source_target_pairs={{0,2},{1,3},{2,0},{3,1},{4,6},{5,7},{6,4},{7,5},{8,10},{9,11},{10,... | collective-permute-start | bytes 393224 | tf_op jit(solution)/shard_map/ppermute | solution.py:217
  98.7 10.8 %collective-permute-start.23 = (bf16[128,512]{1,0:T(8,128)(2,1)S(1)}, bf16[128,512]{1,0:T(8,128)(2,1)S(1)}, u32[]{:S(2)}, u32[]{:S(2)}) collective-permute-start(bf16[128,512]{1,0:T(8,128)(2,1)S(1)} %fusion.10), channel_id=1, source_target_pairs={{0,8},{4,12},{8,0},{12,4},{1,9},{5,13},{9,1},{13,5},{2,10},{6,14},... | collective-permute-start | bytes 393224 | tf_op jit(solution)/shard_map/ppermute | solution.py:208
